TPU v7x, 128 devices: a whole 4x4x4 slice. The times are simulated.
128 devices in a mesh: row: 32 (over x, y, core), col: 4 (over z).
Axes of the slice: x: 4, y: 4, z: 4, core: 2. Of those that a mesh axis runs over, the one named last changes fastest.
Arguments:
- frames: float32 [64, 65536], P(None, ('row', 'col')), may hold values from -8 to 8
- start: float32 [32, 65536], P(None, ('row', 'col')), may hold values from -6 to 6
Outputs:
- basis: float32 [32, 65536], P(None, ('row', 'col'))
All inputs are finite; a program needn't handle non-finite values.
Results may differ from a plain program's by a relative error of at most 0.0003.
Values sent between devices are 32-bit elements; how exact they have to be, the bound alone decides.
A program may use at most 320 MiB of HBM per device.

v0:
```python
import jax
import jax.numpy as jnp
from jax import lax
from jax.sharding import PartitionSpec as P


def build_block(block_points, block_squares, column_points, column_squares):
    products = lax.dot_general(
        block_points, column_points, (((0,), (0,)), ((), ())), precision=lax.Precision.HIGHEST
    )
    distance = block_squares[:, None] + column_squares[None, :] - 2.0 * products
    return jnp.exp(-distance / (0.5 * block_points.shape[0]))


def shards(frames, start):
    block_points = lax.all_gather(frames, "col", axis=1, tiled=True)
    column_points = lax.all_gather(frames, "row", axis=1, tiled=True)
    block_squares = jnp.sum(block_points * block_points, axis=0)
    column_squares = jnp.sum(column_points * column_points, axis=0)
    frame_count = frames.shape[1] * lax.axis_size("row") * lax.axis_size("col")
    block_rows = block_points.shape[1]
    height = min(512, block_rows)
    rounds = block_rows // height

    def kernel_part(index):
        first = index * height
        return build_block(
            block_points[:, first : first + height],
            block_squares[first : first + height],
            column_points,
            column_squares,
        )

    stored = [kernel_part(index) for index in range(rounds)]

    def fetch_tile(index):
        return stored[index]

    def sweep_kernel(spread_weights):
        pieces = []
        for index in range(rounds):
            part = fetch_tile(index)
            if spread_weights is None:
                pieces.append(jnp.sum(part, axis=1)[None, :])
            else:
                pieces.append(
                    lax.dot_general(
                        spread_weights,
                        part,
                        (((1,), (1,)), ((), ())),
                        precision=lax.Precision.HIGHEST,
                    )
                )
        result = jnp.concatenate(pieces, axis=1)
        return result

    def settle(partial_value):
        summed = lax.psum_scatter(partial_value, "col", scatter_dimension=1, tiled=True)
        return summed

    def kernel_product(weights):
        spread_weights = lax.all_gather(weights, "row", axis=1, tiled=True)
        return settle(sweep_kernel(spread_weights))

    def gram_matrix(vectors):
        local_gram = jnp.dot(vectors, vectors.T, precision=lax.Precision.HIGHEST)
        return lax.psum(local_gram, ("row", "col")) / frame_count

    def orthonormal(vectors):
        factor = jnp.linalg.cholesky(gram_matrix(vectors))
        return jax.scipy.linalg.solve_triangular(factor, vectors, lower=True)

    density = settle(sweep_kernel(None))[0]
    inverse = 1.0 / density
    scaled = start * inverse[None, :]
    degree = kernel_product(inverse[None, :])[0]
    product = kernel_product(scaled)
    grown_one = product / degree[None, :]
    basis_one = orthonormal(grown_one)
    grown_two = kernel_product(basis_one * inverse[None, :]) / degree[None, :]
    return orthonormal(grown_two)


def solution(mesh):
    return jax.shard_map(
        shards,
        mesh=mesh,
        in_specs=(P(None, ("row", "col")), P(None, ("row", "col"))),
        out_specs=P(None, ("row", "col")),
        check_vma=False,
    )
```

profile of v0, /device:TPU:1, one launch (start us, length us, event | category | flops | bytes accessed | tf_op | source)
XLA Modules:
  0.0 895.1 jit_solution(2767273097480972749)
XLA Ops:
  7.3 13.6 %all_gather.15 = f32[64,2048]{1,0:T(8,128)S(1)} all-gather(f32[64,512]{1,0:T(8,128)} %param.5), channel_id=1, replica_groups=mesh['row'=32,'col'=4] {'col'}, dimensions={1}, use_global_device_ids=true | all-gather | bytes 655360 | tf_op jit(solution)/shard_map/all_gather | solution.py:16
  21.0 38.4 %all-gather.4.cloned.1.call-done = f32[64,16384]{1,0:T(8,128)} async-done(((f32[64,512]{1,0:T(8,128)}), f32[64,16384]{1,0:T(8,128)}) %all-gather.4.cloned.1.call-update) | async-done | bytes 4194320 | tf_op jit(solution)/shard_map/all_gather | solution.py:17
  59.3 2.7 multiply_reduce_fusion
  62.1 37.7 %fusion.27 = (f32[512]{0:T(512)S(1)}, f32[512,16384]{1,0:T(8,128)}) fusion(f32[64,16384]{1,0:T(8,128)} %all-gather.4.cloned.1.call-done, f32[64,2048]{1,0:T(8,128)S(1)} %all_gather.15, f32[16384]{0:T(1024)S(1)} %multiply_reduce_fusion, f32[512]{0:T(512)S(1)} %get-tuple-element.6), kind=kOutput, calls=%fused_computation.53 | convolution fusion | flops 6492782080 | bytes 37949440 | tf_op jit(solution)/shard_map/dot_general | solution.py:8
  99.8 37.0 %fusion.24 = (f32[512]{0:T(512)S(1)}, f32[512,16384]{1,0:T(8,128)}) fusion(f32[64,16384]{1,0:T(8,128)S(1)} %copy-done.2, f32[64,2048]{1,0:T(8,128)S(1)} %all_gather.15, f32[16384]{0:T(1024)S(1)} %multiply_reduce_fusion, f32[512]{0:T(512)S(1)} %get-tuple-element.8), kind=kOutput, calls=%fused_computation.50 | convolution fusion | flops 6492782080 | bytes 37949440 | tf_op jit(solution)/shard_map/dot_general | solution.py:8
  136.8 36.6 %fusion.25 = (f32[512]{0:T(512)S(1)}, f32[512,16384]{1,0:T(8,128)}) fusion(f32[64,16384]{1,0:T(8,128)S(1)} %copy-done.2, f32[64,2048]{1,0:T(8,128)S(1)} %all_gather.15, f32[16384]{0:T(1024)S(1)} %multiply_reduce_fusion, f32[512]{0:T(512)S(1)} %get-tuple-element.9), kind=kOutput, calls=%fused_computation.51 | convolution fusion | flops 6492782080 | bytes 37949440 | tf_op jit(solution)/shard_map/dot_general | solution.py:8
  173.4 36.7 %fusion.26 = (f32[512]{0:T(512)S(1)}, f32[512,16384]{1,0:T(8,128)}) fusion(f32[64,16384]{1,0:T(8,128)S(1)} %copy-done.2, f32[64,2048]{1,0:T(8,128)S(1)} %all_gather.15, f32[16384]{0:T(1024)S(1)} %multiply_reduce_fusion, f32[512]{0:T(512)S(1)} %get-tuple-element.10), kind=kOutput, calls=%fused_computation.52 | convolution fusion | flops 6492782080 | bytes 37949440 | tf_op jit(solution)/shard_map/dot_general | solution.py:8
  211.6 21.5 %reduce-scatter.13.cloned.1.call-done = f32[512,1]{1,0:T(8,128)} async-done(((f32[2048,1]{1,0:T(8,128)}), f32[512,1]{1,0:T(8,128)}) %reduce-scatter.13.cloned.1.call-update) | async-done | bytes 2064
  234.1 26.0 %all_gather.18 = f32[1,16384]{1,0:T(1,128)S(1)} all-gather(f32[1,512]{1,0:T(1,128)S(1)} %broadcast_divide_fusion.6), channel_id=1, replica_groups=mesh['row'=32,'col'=4] {'row'}, dimensions={1}, use_global_device_ids=true | all-gather | bytes 67584 | tf_op jit(solution)/shard_map/all_gather | solution.py:62
  260.8 31.2 %fusion.8 = f32[1,512]{1,0:T(1,128)S(1)} fusion(f32[512,16384]{1,0:T(8,128)} %get-tuple-element.16, f32[1,16384]{1,0:T(1,128)S(1)} %all_gather.18), kind=kOutput, calls=%fused_computation.17 | convolution fusion | flops 100663296 | bytes 33622016 | tf_op jit(solution)/shard_map/dot_general | solution.py:47
  292.0 30.9 %fusion.6 = f32[1,512]{1,0:T(1,128)S(1)} fusion(f32[512,16384]{1,0:T(8,128)} %get-tuple-element.14, f32[1,16384]{1,0:T(1,128)S(1)} %all_gather.18), kind=kOutput, calls=%fused_computation.15 | convolution fusion | flops 100663296 | bytes 33622016 | tf_op jit(solution)/shard_map/dot_general | solution.py:47
  322.9 31.0 %fusion.4 = f32[1,512]{1,0:T(1,128)S(1)} fusion(f32[512,16384]{1,0:T(8,128)} %get-tuple-element.12, f32[1,16384]{1,0:T(1,128)S(1)} %all_gather.18), kind=kOutput, calls=%fused_computation.13 | convolution fusion | flops 100663296 | bytes 33622016 | tf_op jit(solution)/shard_map/dot_general | solution.py:47
  353.9 30.8 %fusion.10 = f32[1,512]{1,0:T(1,128)S(1)} fusion(f32[512,16384]{1,0:T(8,128)} %get-tuple-element.18, f32[1,16384]{1,0:T(1,128)S(1)} %all_gather.18), kind=kOutput, calls=%fused_computation.19 | convolution fusion | flops 100663296 | bytes 33622016 | tf_op jit(solution)/shard_map/dot_general | solution.py:47
  386.2 34.4 %fusion.31 = f32[32,512]{1,0:T(8,128)S(1)} fusion(f32[32,16384]{1,0:T(8,128)} %all-gather.6.cloned.1.call-done, f32[512,16384]{1,0:T(8,128)} %get-tuple-element.12), kind=kOutput, calls=%fused_computation.57 | convolution fusion | flops 3221225472 | bytes 35717120 | tf_op jit(solution)/shard_map/dot_general | solution.py:47
  420.5 33.9 %fusion.30 = f32[32,512]{1,0:T(8,128)S(1)} fusion(f32[32,16384]{1,0:T(8,128)S(1)} %copy-done, f32[512,16384]{1,0:T(8,128)} %get-tuple-element.14), kind=kOutput, calls=%fused_computation.56 | convolution fusion | flops 3221225472 | bytes 35717120 | tf_op jit(solution)/shard_map/dot_general | solution.py:47
  454.4 34.3 %fusion.29 = f32[32,512]{1,0:T(8,128)S(1)} fusion(f32[32,16384]{1,0:T(8,128)S(1)} %copy-done, f32[512,16384]{1,0:T(8,128)} %get-tuple-element.16), kind=kOutput, calls=%fused_computation.55 | convolution fusion | flops 3221225472 | bytes 35717120 | tf_op jit(solution)/shard_map/dot_general | solution.py:47
  488.8 33.9 %fusion.28 = f32[32,512]{1,0:T(8,128)S(1)} fusion(f32[32,16384]{1,0:T(8,128)S(1)} %copy-done, f32[512,16384]{1,0:T(8,128)} %get-tuple-element.18), kind=kOutput, calls=%fused_computation.54 | convolution fusion | flops 3221225472 | bytes 35717120 | tf_op jit(solution)/shard_map/dot_general | solution.py:47
  524.5 14.8 %reduce-scatter.9.cloned.1.call-done = f32[32,512]{1,0:T(8,128)} async-done(((f32[32,2048]{1,0:T(8,128)}), f32[32,512]{1,0:T(8,128)}) %reduce-scatter.9.cloned.1.call-update) | async-done | bytes 65552 | tf_op jit(solution)/shard_map/reduce_scatter | solution.py:58
  540.4 67.2 %psum.14 = f32[32,32]{0,1:T(8,128)S(1)} all-reduce(f32[32,32]{0,1:T(8,128)S(1)} %fusion.12), channel_id=1, replica_groups=mesh['row'=32,'col'=4] {'row','col'}, use_global_device_ids=true, to_apply=%region_9.0 | all-reduce | flops 1024 | bytes 8192 | tf_op jit(solution)/shard_map/psum | solution.py:67
  607.7 2.9 cholesky.44
  611.9 2.4 custom-call.6
  614.4 1.8 convolution_multiply_fusion
  616.2 40.7 %all-gather.8.cloned.1.call-done = f32[32,16384]{1,0:T(8,128)} async-done(((f32[32,512]{1,0:T(8,128)}), f32[32,16384]{1,0:T(8,128)}) %all-gather.8.cloned.1.call-update) | async-done | bytes 2097168 | tf_op jit(solution)/shard_map/all_gather | solution.py:62
  656.8 34.2 %fusion.35 = f32[32,512]{1,0:T(8,128)S(1)} fusion(f32[32,16384]{1,0:T(8,128)} %all-gather.8.cloned.1.call-done, f32[512,16384]{1,0:T(8,128)} %get-tuple-element.12), kind=kOutput, calls=%fused_computation.61 | convolution fusion | flops 3221225472 | bytes 35717120 | tf_op jit(solution)/shard_map/dot_general | solution.py:47
  691.0 33.9 %fusion.34 = f32[32,512]{1,0:T(8,128)S(1)} fusion(f32[32,16384]{1,0:T(8,128)S(1)} %copy-done.1, f32[512,16384]{1,0:T(8,128)} %get-tuple-element.14), kind=kOutput, calls=%fused_computation.60 | convolution fusion | flops 3221225472 | bytes 35717120 | tf_op jit(solution)/shard_map/dot_general | solution.py:47
  724.9 34.1 %fusion.33 = f32[32,512]{1,0:T(8,128)S(1)} fusion(f32[32,16384]{1,0:T(8,128)S(1)} %copy-done.1, f32[512,16384]{1,0:T(8,128)} %get-tuple-element.16), kind=kOutput, calls=%fused_computation.59 | convolution fusion | flops 3221225472 | bytes 35717120 | tf_op jit(solution)/shard_map/dot_general | solution.py:47
  759.0 33.9 %fusion.32 = f32[32,512]{1,0:T(8,128)S(1)} fusion(f32[32,16384]{1,0:T(8,128)S(1)} %copy-done.1, f32[512,16384]{1,0:T(8,128)} %get-tuple-element.18), kind=kOutput, calls=%fused_computation.58 | convolution fusion | flops 3221225472 | bytes 35717120 | tf_op jit(solution)/shard_map/dot_general | solution.py:47
  793.6 17.6 %reduce-scatter.11.cloned.1.call-done = f32[32,512]{1,0:T(8,128)} async-done(((f32[32,2048]{1,0:T(8,128)}), f32[32,512]{1,0:T(8,128)}) %reduce-scatter.11.cloned.1.call-update) | async-done | bytes 65552 | tf_op jit(solution)/shard_map/reduce_scatter | solution.py:58
  812.3 67.0 %psum.15 = f32[32,32]{0,1:T(8,128)S(1)} all-reduce(f32[32,32]{0,1:T(8,128)S(1)} %fusion.14), channel_id=1, replica_groups=mesh['row'=32,'col'=4] {'row','col'}, use_global_device_ids=true, to_apply=%region_13.16 | all-reduce | flops 1024 | bytes 8192 | tf_op jit(solution)/shard_map/psum | solution.py:67
  879.4 2.9 cholesky.55
  883.7 2.4 custom-call.7
  886.1 1.8 fusion.13
  (50 shorter events, 13.2 us)
Async XLA Ops:
  6.5 52.8 %all-gather.4.cloned.1.call-start = ((), (), s32[]{:S(2)}) async-start(), calls=%async_computation.4 | async-start | bytes 4325376 | tf_op jit(solution)/shard_map/all_gather | solution.py:17
  7.3 225.8 %reduce-scatter.13.cloned.1.call-start = ((), (), s32[]{:S(2)}) async-start(), calls=%async_computation.9 | async-start | bytes 1310720
  59.3 40.5 %copy-start.2 = (f32[64,16384]{1,0:T(8,128)S(1)}, f32[64,16384]{1,0:T(8,128)}, u32[]{:S(2)}) copy-start(f32[64,16384]{1,0:T(8,128)} %all-gather.4.cloned.1.call-done) | copy-start | bytes 12582916
  173.4 86.7 %copy-start.3 = (f32[32,512]{1,0:T(8,128)S(1)}, f32[32,512]{1,0:T(8,128)}, u32[]{:S(2)}) copy-start(f32[32,512]{1,0:T(8,128)} %param.6) | copy-start | bytes 196612
  211.5 174.6 %all-gather.6.cloned.1.call-start = ((), (), s32[]{:S(2)}) async-start(), calls=%async_computation.5 | async-start | bytes 2162688 | tf_op jit(solution)/shard_map/all_gather | solution.py:62
  260.8 262.7 %reduce-scatter.15.cloned.1.call-start = ((), (), s32[]{:S(2)}) async-start(), calls=%async_computation.10 | async-start | bytes 1310720
  386.1 153.2 %reduce-scatter.9.cloned.1.call-start = ((), (), s32[]{:S(2)}) async-start(), calls=%async_computation.6 | async-start | bytes 327680 | tf_op jit(solution)/shard_map/reduce_scatter | solution.py:58
  386.1 34.4 %copy-start = (f32[32,16384]{1,0:T(8,128)S(1)}, f32[32,16384]{1,0:T(8,128)}, u32[]{:S(2)}) copy-start(f32[32,16384]{1,0:T(8,128)} %all-gather.6.cloned.1.call-done) | copy-start | bytes 6291460
  523.4 133.5 %all-gather.8.cloned.1.call-start = ((), (), s32[]{:S(2)}) async-start(), calls=%async_computation.7 | async-start | bytes 2162688 | tf_op jit(solution)/shard_map/all_gather | solution.py:62
  616.1 195.1 %reduce-scatter.11.cloned.1.call-start = ((), (), s32[]{:S(2)}) async-start(), calls=%async_computation.8 | async-start | bytes 327680 | tf_op jit(solution)/shard_map/reduce_scatter | solution.py:58
  656.8 34.2 %copy-start.1 = (f32[32,16384]{1,0:T(8,128)S(1)}, f32[32,16384]{1,0:T(8,128)}, u32[]{:S(2)}) copy-start(f32[32,16384]{1,0:T(8,128)} %all-gather.8.cloned.1.call-done) | copy-start | bytes 6291460
Sparse Core Ops, SparseCore 0:
  9.7 49.5 all-gather.3
  211.6 21.3 reduce-scatter.12
  260.9 41.3 all-gather.5
  386.2 19.1 reduce-scatter.14
  523.5 15.7 reduce-scatter.8
  616.3 40.5 all-gather.7
  793.7 17.4 reduce-scatter.10
where the time goes:
time: 902 us; the launch traced here: 895 us
  matrix products  550 us (61%)
  blocking collectives  174 us (19%)
  waiting for transfers between devices  134 us (15%)
  other arithmetic  18.3 us (2%)
  between operations  14 us (2%)
    dot_general x12, matrix products, sweep_kernel(): lax.dot_general(spread_weights, part, (((1,), (1,)), ((), ())), precision...  396 us
    dot_general x4, matrix products, build_block(): lax.dot_general(block_points, column_points, (((0,), (0,)), ((), ())), pr...  148 us
    psum x2, blocking collectives, gram_matrix(): return lax.psum(local_gram, ('row', 'col')) / frame_count  134 us
    all_gather x2, waiting for transfers between devices, kernel_product(): spread_weights = lax.all_gather(weights, 'row', axis=1, tiled=True)  40.7 us
    all_gather x1, waiting for transfers between devices, shards(): column_points = lax.all_gather(frames, 'row', axis=1, tiled=True)  38.4 us
    reduce_scatter x2, waiting for transfers between devices, settle(): lax.psum_scatter(partial_value, 'col', scatter_dimension=1, tiled=True)  32.4 us
    all_gather x1, blocking collectives, kernel_product(): spread_weights = lax.all_gather(weights, 'row', axis=1, tiled=True)  26 us
    unnamed x9, waiting for transfers between devices  22.3 us
  transfers between devices with their start and end apart: 7, of which 5 were waited for; matrix products, arithmetic and copies ran while one was open for 29% of the time, Pallas kernels for 0%

commit v1 on v0

--- a/solution.py
+++ b/solution.py
@@ -64,7 +64,7 @@
 
     def gram_matrix(vectors):
         local_gram = jnp.dot(vectors, vectors.T, precision=lax.Precision.HIGHEST)
-        return lax.psum(local_gram, ("row", "col")) / frame_count
+        return lax.psum(lax.psum(local_gram, "col"), "row") / frame_count
 
     def orthonormal(vectors):
         factor = jnp.linalg.cholesky(gram_matrix(vectors))

time: 902 us -> 1050 us (1.16)
  blocking collectives: 174 us -> 312 us
    psum x2 -> x4, blocking collectives: 134 us -> 272 us  [gram_matrix(): return lax.psum(lax.psum(local_gram, 'col'), 'row') / frame_count]
  transfers between devices with their start and end apart: 7 -> 7, of which waited for: 5 -> 5; matrix products, arithmetic and copies ran while one was open for 29% -> 25% of each run, Pallas kernels for 0% -> 0%
where the time goes in v1:
time: 1050 us; the launch traced here: 1040 us
  matrix products  550 us (52%)
  blocking collectives  312 us (30%)
  waiting for transfers between devices  136 us (13%)
  other arithmetic  18.3 us (2%)
  between operations  13.9 us (1%)
    dot_general x12, matrix products, sweep_kernel(): lax.dot_general(spread_weights, part, (((1,), (1,)), ((), ())), precision...  396 us
    psum x4, blocking collectives, gram_matrix(): return lax.psum(lax.psum(local_gram, 'col'), 'row') / frame_count  272 us
    dot_general x4, matrix products, build_block(): lax.dot_general(block_points, column_points, (((0,), (0,)), ((), ())), pr...  148 us
    all_gather x2, waiting for transfers between devices, kernel_product(): spread_weights = lax.all_gather(weights, 'row', axis=1, tiled=True)  43.4 us
    all_gather x1, waiting for transfers between devices, shards(): column_points = lax.all_gather(frames, 'row', axis=1, tiled=True)  38.4 us
    reduce_scatter x2, waiting for transfers between devices, settle(): lax.psum_scatter(partial_value, 'col', scatter_dimension=1, tiled=True)  32.4 us
    all_gather x1, blocking collectives, kernel_product(): spread_weights = lax.all_gather(weights, 'row', axis=1, tiled=True)  26 us
    unnamed x9, waiting for transfers between devices  22.3 us
  transfers between devices with their start and end apart: 7, of which 5 were waited for; matrix products, arithmetic and copies ran while one was open for 25% of the time, Pallas kernels for 0%

profile of v1, /device:TPU:1, one launch (start us, length us, event | category | flops | bytes accessed | tf_op | source)
XLA Modules:
  0.0 1035.5 jit_solution(16084491066478499335)
XLA Ops:
  7.3 13.6 %all_gather.15 = f32[64,2048]{1,0:T(8,128)S(1)} all-gather(f32[64,512]{1,0:T(8,128)} %param.5), channel_id=1, replica_groups=mesh['row'=32,'col'=4] {'col'}, dimensions={1}, use_global_device_ids=true | all-gather | bytes 655360 | tf_op jit(solution)/shard_map/all_gather | solution.py:16
  21.0 38.4 %all-gather.4.cloned.1.call-done = f32[64,16384]{1,0:T(8,128)} async-done(((f32[64,512]{1,0:T(8,128)}), f32[64,16384]{1,0:T(8,128)}) %all-gather.4.cloned.1.call-update) | async-done | bytes 4194320 | tf_op jit(solution)/shard_map/all_gather | solution.py:17
  59.3 2.7 multiply_reduce_fusion
  62.1 37.7 %fusion.27 = (f32[512]{0:T(512)S(1)}, f32[512,16384]{1,0:T(8,128)}) fusion(f32[64,16384]{1,0:T(8,128)} %all-gather.4.cloned.1.call-done, f32[64,2048]{1,0:T(8,128)S(1)} %all_gather.15, f32[16384]{0:T(1024)S(1)} %multiply_reduce_fusion, f32[512]{0:T(512)S(1)} %get-tuple-element.6), kind=kOutput, calls=%fused_computation.53 | convolution fusion | flops 6492782080 | bytes 37949440 | tf_op jit(solution)/shard_map/dot_general | solution.py:8
  99.8 37.0 %fusion.24 = (f32[512]{0:T(512)S(1)}, f32[512,16384]{1,0:T(8,128)}) fusion(f32[64,16384]{1,0:T(8,128)S(1)} %copy-done.2, f32[64,2048]{1,0:T(8,128)S(1)} %all_gather.15, f32[16384]{0:T(1024)S(1)} %multiply_reduce_fusion, f32[512]{0:T(512)S(1)} %get-tuple-element.8), kind=kOutput, calls=%fused_computation.50 | convolution fusion | flops 6492782080 | bytes 37949440 | tf_op jit(solution)/shard_map/dot_general | solution.py:8
  136.8 36.6 %fusion.25 = (f32[512]{0:T(512)S(1)}, f32[512,16384]{1,0:T(8,128)}) fusion(f32[64,16384]{1,0:T(8,128)S(1)} %copy-done.2, f32[64,2048]{1,0:T(8,128)S(1)} %all_gather.15, f32[16384]{0:T(1024)S(1)} %multiply_reduce_fusion, f32[512]{0:T(512)S(1)} %get-tuple-element.9), kind=kOutput, calls=%fused_computation.51 | convolution fusion | flops 6492782080 | bytes 37949440 | tf_op jit(solution)/shard_map/dot_general | solution.py:8
  173.4 36.7 %fusion.26 = (f32[512]{0:T(512)S(1)}, f32[512,16384]{1,0:T(8,128)}) fusion(f32[64,16384]{1,0:T(8,128)S(1)} %copy-done.2, f32[64,2048]{1,0:T(8,128)S(1)} %all_gather.15, f32[16384]{0:T(1024)S(1)} %multiply_reduce_fusion, f32[512]{0:T(512)S(1)} %get-tuple-element.10), kind=kOutput, calls=%fused_computation.52 | convolution fusion | flops 6492782080 | bytes 37949440 | tf_op jit(solution)/shard_map/dot_general | solution.py:8
  211.6 21.5 %reduce-scatter.13.cloned.1.call-done = f32[512,1]{1,0:T(8,128)} async-done(((f32[2048,1]{1,0:T(8,128)}), f32[512,1]{1,0:T(8,128)}) %reduce-scatter.13.cloned.1.call-update) | async-done | bytes 2064
  234.1 26.0 %all_gather.18 = f32[1,16384]{1,0:T(1,128)S(1)} all-gather(f32[1,512]{1,0:T(1,128)S(1)} %broadcast_divide_fusion.6), channel_id=1, replica_groups=mesh['row'=32,'col'=4] {'row'}, dimensions={1}, use_global_device_ids=true | all-gather | bytes 67584 | tf_op jit(solution)/shard_map/all_gather | solution.py:62
  260.8 31.2 %fusion.8 = f32[1,512]{1,0:T(1,128)S(1)} fusion(f32[512,16384]{1,0:T(8,128)} %get-tuple-element.16, f32[1,16384]{1,0:T(1,128)S(1)} %all_gather.18), kind=kOutput, calls=%fused_computation.17 | convolution fusion | flops 100663296 | bytes 33622016 | tf_op jit(solution)/shard_map/dot_general | solution.py:47
  292.0 30.9 %fusion.6 = f32[1,512]{1,0:T(1,128)S(1)} fusion(f32[512,16384]{1,0:T(8,128)} %get-tuple-element.14, f32[1,16384]{1,0:T(1,128)S(1)} %all_gather.18), kind=kOutput, calls=%fused_computation.15 | convolution fusion | flops 100663296 | bytes 33622016 | tf_op jit(solution)/shard_map/dot_general | solution.py:47
  322.9 31.0 %fusion.4 = f32[1,512]{1,0:T(1,128)S(1)} fusion(f32[512,16384]{1,0:T(8,128)} %get-tuple-element.12, f32[1,16384]{1,0:T(1,128)S(1)} %all_gather.18), kind=kOutput, calls=%fused_computation.13 | convolution fusion | flops 100663296 | bytes 33622016 | tf_op jit(solution)/shard_map/dot_general | solution.py:47
  353.9 30.8 %fusion.10 = f32[1,512]{1,0:T(1,128)S(1)} fusion(f32[512,16384]{1,0:T(8,128)} %get-tuple-element.18, f32[1,16384]{1,0:T(1,128)S(1)} %all_gather.18), kind=kOutput, calls=%fused_computation.19 | convolution fusion | flops 100663296 | bytes 33622016 | tf_op jit(solution)/shard_map/dot_general | solution.py:47
  386.2 34.4 %fusion.31 = f32[32,512]{1,0:T(8,128)S(1)} fusion(f32[32,16384]{1,0:T(8,128)} %all-gather.6.cloned.1.call-done, f32[512,16384]{1,0:T(8,128)} %get-tuple-element.12), kind=kOutput, calls=%fused_computation.57 | convolution fusion | flops 3221225472 | bytes 35717120 | tf_op jit(solution)/shard_map/dot_general | solution.py:47
  420.5 33.9 %fusion.30 = f32[32,512]{1,0:T(8,128)S(1)} fusion(f32[32,16384]{1,0:T(8,128)S(1)} %copy-done, f32[512,16384]{1,0:T(8,128)} %get-tuple-element.14), kind=kOutput, calls=%fused_computation.56 | convolution fusion | flops 3221225472 | bytes 35717120 | tf_op jit(solution)/shard_map/dot_general | solution.py:47
  454.4 34.3 %fusion.29 = f32[32,512]{1,0:T(8,128)S(1)} fusion(f32[32,16384]{1,0:T(8,128)S(1)} %copy-done, f32[512,16384]{1,0:T(8,128)} %get-tuple-element.16), kind=kOutput, calls=%fused_computation.55 | convolution fusion | flops 3221225472 | bytes 35717120 | tf_op jit(solution)/shard_map/dot_general | solution.py:47
  488.8 33.9 %fusion.28 = f32[32,512]{1,0:T(8,128)S(1)} fusion(f32[32,16384]{1,0:T(8,128)S(1)} %copy-done, f32[512,16384]{1,0:T(8,128)} %get-tuple-element.18), kind=kOutput, calls=%fused_computation.54 | convolution fusion | flops 3221225472 | bytes 35717120 | tf_op jit(solution)/shard_map/dot_general | solution.py:47
  524.5 14.8 %reduce-scatter.9.cloned.1.call-done = f32[32,512]{1,0:T(8,128)} async-done(((f32[32,2048]{1,0:T(8,128)}), f32[32,512]{1,0:T(8,128)}) %reduce-scatter.9.cloned.1.call-update) | async-done | bytes 65552 | tf_op jit(solution)/shard_map/reduce_scatter | solution.py:58
  540.4 12.0 %psum.28 = f32[32,32]{0,1:T(8,128)S(1)} all-reduce(f32[32,32]{0,1:T(8,128)S(1)} %fusion.12), channel_id=1, replica_groups=mesh['row'=32,'col'=4] {'col'}, use_global_device_ids=true, to_apply=%region_9.0 | all-reduce | flops 1024 | bytes 8192 | tf_op jit(solution)/shard_map/psum | solution.py:67
  552.4 124.2 %psum.29 = f32[32,32]{0,1:T(8,128)S(1)} all-reduce(f32[32,32]{0,1:T(8,128)S(1)} %psum.28), channel_id=1, replica_groups=mesh['row'=32,'col'=4] {'row'}, use_global_device_ids=true, to_apply=%region_10.0 | all-reduce | flops 1024 | bytes 8192 | tf_op jit(solution)/shard_map/psum | solution.py:67
  676.7 2.9 cholesky.44
  680.9 2.4 custom-call.6
  685.2 43.3 %all-gather.8.cloned.1.call-done = f32[32,16384]{1,0:T(8,128)} async-done(((f32[32,512]{1,0:T(8,128)}), f32[32,16384]{1,0:T(8,128)}) %all-gather.8.cloned.1.call-update) | async-done | bytes 2097168 | tf_op jit(solution)/shard_map/all_gather | solution.py:62
  728.5 34.2 %fusion.35 = f32[32,512]{1,0:T(8,128)S(1)} fusion(f32[32,16384]{1,0:T(8,128)} %all-gather.8.cloned.1.call-done, f32[512,16384]{1,0:T(8,128)} %get-tuple-element.12), kind=kOutput, calls=%fused_computation.61 | convolution fusion | flops 3221225472 | bytes 35717120 | tf_op jit(solution)/shard_map/dot_general | solution.py:47
  762.7 33.9 %fusion.34 = f32[32,512]{1,0:T(8,128)S(1)} fusion(f32[32,16384]{1,0:T(8,128)S(1)} %copy-done.1, f32[512,16384]{1,0:T(8,128)} %get-tuple-element.14), kind=kOutput, calls=%fused_computation.60 | convolution fusion | flops 3221225472 | bytes 35717120 | tf_op jit(solution)/shard_map/dot_general | solution.py:47
  796.6 34.1 %fusion.33 = f32[32,512]{1,0:T(8,128)S(1)} fusion(f32[32,16384]{1,0:T(8,128)S(1)} %copy-done.1, f32[512,16384]{1,0:T(8,128)} %get-tuple-element.16), kind=kOutput, calls=%fused_computation.59 | convolution fusion | flops 3221225472 | bytes 35717120 | tf_op jit(solution)/shard_map/dot_general | solution.py:47
  830.7 33.9 %fusion.32 = f32[32,512]{1,0:T(8,128)S(1)} fusion(f32[32,16384]{1,0:T(8,128)S(1)} %copy-done.1, f32[512,16384]{1,0:T(8,128)} %get-tuple-element.18), kind=kOutput, calls=%fused_computation.58 | convolution fusion | flops 3221225472 | bytes 35717120 | tf_op jit(solution)/shard_map/dot_general | solution.py:47
  865.3 17.6 %reduce-scatter.11.cloned.1.call-done = f32[32,512]{1,0:T(8,128)} async-done(((f32[32,2048]{1,0:T(8,128)}), f32[32,512]{1,0:T(8,128)}) %reduce-scatter.11.cloned.1.call-update) | async-done | bytes 65552 | tf_op jit(solution)/shard_map/reduce_scatter | solution.py:58
  884.0 11.7 %psum.30 = f32[32,32]{0,1:T(8,128)S(1)} all-reduce(f32[32,32]{0,1:T(8,128)S(1)} %fusion.14), channel_id=1, replica_groups=mesh['row'=32,'col'=4] {'col'}, use_global_device_ids=true, to_apply=%region_14.17 | all-reduce | flops 1024 | bytes 8192 | tf_op jit(solution)/shard_map/psum | solution.py:67
  895.8 124.2 %psum.31 = f32[32,32]{0,1:T(8,128)S(1)} all-reduce(f32[32,32]{0,1:T(8,128)S(1)} %psum.30), channel_id=1, replica_groups=mesh['row'=32,'col'=4] {'row'}, use_global_device_ids=true, to_apply=%region_15.18 | all-reduce | flops 1024 | bytes 8192 | tf_op jit(solution)/shard_map/psum | solution.py:67
  1020.0 2.9 cholesky.55
  1024.3 2.4 custom-call.7
  (52 shorter events, 16.7 us)
Async XLA Ops:
  6.5 52.8 %all-gather.4.cloned.1.call-start = ((), (), s32[]{:S(2)}) async-start(), calls=%async_computation.4 | async-start | bytes 4325376 | tf_op jit(solution)/shard_map/all_gather | solution.py:17
  7.3 225.8 %reduce-scatter.13.cloned.1.call-start = ((), (), s32[]{:S(2)}) async-start(), calls=%async_computation.9 | async-start | bytes 1310720
  59.3 40.5 %copy-start.2 = (f32[64,16384]{1,0:T(8,128)S(1)}, f32[64,16384]{1,0:T(8,128)}, u32[]{:S(2)}) copy-start(f32[64,16384]{1,0:T(8,128)} %all-gather.4.cloned.1.call-done) | copy-start | bytes 12582916
  173.4 86.7 %copy-start.3 = (f32[32,512]{1,0:T(8,128)S(1)}, f32[32,512]{1,0:T(8,128)}, u32[]{:S(2)}) copy-start(f32[32,512]{1,0:T(8,128)} %param.6) | copy-start | bytes 196612
  211.5 174.6 %all-gather.6.cloned.1.call-start = ((), (), s32[]{:S(2)}) async-start(), calls=%async_computation.5 | async-start | bytes 2162688 | tf_op jit(solution)/shard_map/all_gather | solution.py:62
  260.8 262.7 %reduce-scatter.15.cloned.1.call-start = ((), (), s32[]{:S(2)}) async-start(), calls=%async_computation.10 | async-start | bytes 1310720
  386.1 153.2 %reduce-scatter.9.cloned.1.call-start = ((), (), s32[]{:S(2)}) async-start(), calls=%async_computation.6 | async-start | bytes 327680 | tf_op jit(solution)/shard_map/reduce_scatter | solution.py:58
  386.1 34.4 %copy-start = (f32[32,16384]{1,0:T(8,128)S(1)}, f32[32,16384]{1,0:T(8,128)}, u32[]{:S(2)}) copy-start(f32[32,16384]{1,0:T(8,128)} %all-gather.6.cloned.1.call-done) | copy-start | bytes 6291460
  523.4 205.2 %all-gather.8.cloned.1.call-start = ((), (), s32[]{:S(2)}) async-start(), calls=%async_computation.7 | async-start | bytes 2162688 | tf_op jit(solution)/shard_map/all_gather | solution.py:62
  685.1 197.8 %reduce-scatter.11.cloned.1.call-start = ((), (), s32[]{:S(2)}) async-start(), calls=%async_computation.8 | async-start | bytes 327680 | tf_op jit(solution)/shard_map/reduce_scatter | solution.py:58
  728.5 34.2 %copy-start.1 = (f32[32,16384]{1,0:T(8,128)S(1)}, f32[32,16384]{1,0:T(8,128)}, u32[]{:S(2)}) copy-start(f32[32,16384]{1,0:T(8,128)} %all-gather.8.cloned.1.call-done) | copy-start | bytes 6291460
Sparse Core Ops, SparseCore 0:
  9.7 49.5 all-gather.3
  211.6 21.3 reduce-scatter.12
  260.9 41.3 all-gather.5
  386.2 19.1 reduce-scatter.14
  523.5 15.7 reduce-scatter.8
  685.3 43.2 all-gather.7
  865.4 17.4 reduce-scatter.10
